TPU v7x, 256 devices: a whole 4x4x8 slice. The times are simulated.
256 devices in a mesh: user: 8 (over y, x_lo), item: 32 (over z, x_hi, core).
Axes of the slice: x: 4 (x_hi: 2, x_lo: 2; x = x_hi * 2 + x_lo), y: 4, z: 8, core: 2. Of those that a mesh axis runs over, the one named last changes fastest.
Arguments:
- user_panel: bfloat16 [2048, 1024], P(('user', 'item')), may hold values from -6 to 6
- attr_panel: bfloat16 [2048, 1024], P(('user', 'item')), may hold values from -6 to 6
- user_blocks: bfloat16 [128, 4096, 128], P('user', 'item'), may hold values from -6 to 6
- user_rows: int32 [128, 32], P('user', 'item'), may hold values from 0 to 1
- user_cols: int32 [128, 32], P('user', 'item'), may hold values from 0 to 24
- attr_blocks: bfloat16 [128, 4096, 128], P('user', 'item'), may hold values from -6 to 6
- attr_rows: int32 [128, 32], P('user', 'item'), may hold values from 0 to 1
- attr_cols: int32 [128, 32], P('user', 'item'), may hold values from 0 to 24
Outputs:
- band_tail: float32 [1024, 102400], P('user', 'item')
- band_self: float32 [1024, 1024], P('user', 'item')
All inputs are finite; a program needn't handle non-finite values.
Results may differ from a plain program's by a relative error of at most 0.012.
Values may be sent and summed in bfloat16 or wider, within the bound.
A program may use at most 64 MiB of HBM per device.

v0:
```python
import jax
import jax.numpy as jnp
from jax import lax
from jax.sharding import Mesh
from jax.sharding import PartitionSpec as P

ITEM_DEV = 3200
USER = ("user_0", "user_1")
USER_ITEM = ("user_0", "user_1", "item")


alpha_weight = 0.5
ridge = 1.0


def sent_together(arrays, axis, dim, along):
    both = jnp.concatenate(arrays, axis=along)
    result, at, outs = (lax.all_gather(both, axis, axis=dim, tiled=True), 0, [])
    for a in arrays:
        outs.append(lax.slice_in_dim(result, at, at + a.shape[along], axis=along))
        at += a.shape[along]
    return tuple(outs)


def over_axes(value, axes):
    for axis in axes:
        value = lax.psum(value, axis)
    return value


def own_rows(terms, axes):
    subtotal = terms.astype(jnp.bfloat16)
    for axis in axes:
        subtotal = lax.psum_scatter(subtotal, axis, scatter_dimension=0, tiled=True)
    return subtotal.astype(jnp.float32)


def in_blocks(value, dim, count):
    before, after = (value.shape[:dim], value.shape[dim + 1 :])
    return jnp.moveaxis(value.reshape(*before, count, -1, *after), dim, 0)


def sum_at_owner(value, axis, dim):
    tiles = in_blocks(value, dim, lax.axis_size(axis))
    arrived = lax.all_to_all(tiles, axis, split_axis=0, concat_axis=0, tiled=True)
    return arrived.astype(jnp.float32).sum(axis=0)


def dense_local(blocks, rows, cols, row_blocks, item_width):
    side = blocks.shape[-1]
    item_blocks = item_width // side
    start = jnp.zeros((row_blocks, side, item_blocks, side), jnp.float32)
    dense = start.at[rows, :, cols, :].add(blocks.astype(jnp.float32))
    return dense.reshape(row_blocks * side, item_width).astype(jnp.bfloat16)


def local(
    user_panel, attr_panel, user_blocks, user_rows, user_cols, attr_blocks, attr_rows, attr_cols
):
    users, attrs = sent_together((user_panel, attr_panel), "item", 0, 1)
    band_width = users.shape[1]
    side = user_blocks.shape[-1]
    item_width = ITEM_DEV
    user_dense = dense_local(
        user_blocks,
        user_rows.reshape(-1),
        user_cols.reshape(-1),
        users.shape[0] // side,
        item_width,
    )
    attr_dense = dense_local(
        attr_blocks,
        attr_rows.reshape(-1),
        attr_cols.reshape(-1),
        attrs.shape[0] // side,
        item_width,
    )
    usersf = users.astype(jnp.float32)
    attrsf = attrs.astype(jnp.float32)
    local_weight = jnp.sum(usersf * usersf, axis=0) + alpha_weight * jnp.sum(
        attrsf * attrsf, axis=0
    )
    weight = over_axes(local_weight, USER)
    width = band_width // lax.axis_size("item")
    col_first = lax.axis_index("item") * width
    user_slice = lax.dynamic_slice_in_dim(users, col_first, width, 1)
    attr_slice = lax.dynamic_slice_in_dim(attrs, col_first, width, 1)
    contract = (((0,), (0,)), ((), ()))
    self_part = lax.dot_general(
        users, user_slice, contract, preferred_element_type=jnp.float32
    ) + alpha_weight * lax.dot_general(
        attrs, attr_slice, contract, preferred_element_type=jnp.float32
    )
    gram_tail = own_rows(
        lax.dot_general(users, user_dense, contract, preferred_element_type=jnp.float32)
        + alpha_weight
        * lax.dot_general(attrs, attr_dense, contract, preferred_element_type=jnp.float32),
        USER,
    )
    gram_self = sum_at_owner(self_part.astype(jnp.bfloat16), USER, 0)
    row_count = band_width // lax.axis_size(USER)
    row_first = lax.axis_index(USER) * row_count
    scale = lax.rsqrt(lax.dynamic_slice_in_dim(weight, row_first, row_count) + ridge)
    band_tail = gram_tail * scale[:, None]
    row_ids = row_first + lax.broadcasted_iota(jnp.int32, (row_count, width), 0)
    col_ids = col_first + lax.broadcasted_iota(jnp.int32, (row_count, width), 1)
    band_self = jnp.where(row_ids == col_ids, jnp.float32(0.0), gram_self * scale[:, None])
    return (band_tail, band_self)


def solution(mesh):
    finer = Mesh(mesh.devices.reshape(4, 2, mesh.shape["item"]), ("user_0", "user_1", "item"))
    return jax.shard_map(
        local,
        mesh=finer,
        in_specs=(
            P(USER_ITEM, None),
            P(USER_ITEM, None),
            P(USER, "item", None),
            P(USER, "item"),
            P(USER, "item"),
            P(USER, "item", None),
            P(USER, "item"),
            P(USER, "item"),
        ),
        out_specs=(P(USER, "item"), P(USER, "item")),
        check_vma=False,
    )
```

profile of v0, /device:TPU:1, one launch (start us, length us, event | category | flops | bytes accessed | tf_op | source)
XLA Modules:
  0.0 210.7 jit_solution(3696035373219874829)
XLA Ops:
  7.2 0.0 all-gather.2.cloned.1.call-start
  7.2 1.3 pad_maximum_fusion
  8.5 0.0 all-gather.2.cloned.1.call-update
  8.6 0.0 reduce-scatter.3.cloned.1.call-start
  8.6 2.1 %convert_element_type.36 = f32[16,128,128]{2,1,0:T(8,128)} convert(bf16[16,128,128]{2,1,0:T(8,128)(2,1)} %param.10) | non-fusion elementwise | flops 262144 | bytes 1572864 | tf_op jit(solution)/shard_map/convert_element_type | solution.py:53
  10.7 0.7 fusion.15
  11.5 0.4 broadcast.25.clone
  11.8 2.9 %scatter_fusion = f32[2,128,25,128]{3,1,2,0:T(8,128)S(1)} fusion(f32[2,128,25,128]{3,1,2,0:T(8,128)S(1)} %broadcast.25.clone, s32[16]{0:T(128)S(1)} %get-tuple-element.6, f32[16,128,128]{2,1,0:T(8,128)} %convert_element_type.36), kind=kCustom, calls=%fused_computation | custom fusion | flops 262144 | bytes 3145856 | tf_op jit(solution)/shard_map/scatter-add | solution.py:53
  14.7 1.4 convert_element_type.37
  16.2 0.0 copy-start.2
  16.2 5.4 %copy.12 = bf16[2,128,25,128]{1,0,3,2:T(2,128)(2,1)} copy(bf16[2,128,25,128]{3,1,2,0:T(8,128)(2,1)} %convert_element_type.37) | data formatting | bytes 3276800 | tf_op jit(solution)/shard_map/convert_element_type | solution.py:54
  21.6 0.0 copy-done.2
  21.6 1.1 convert_element_type.39
  22.6 0.4 broadcast.25.clone.1
  23.0 2.9 %scatter_fusion.1 = f32[2,128,25,128]{3,1,2,0:T(8,128)S(1)} fusion(f32[2,128,25,128]{3,1,2,0:T(8,128)S(1)} %broadcast.25.clone.1, s32[16]{0:T(128)S(1)} %get-tuple-element.7, f32[16,128,128]{2,1,0:T(8,128)} %convert_element_type.39), kind=kCustom, calls=%fused_computation.1 | custom fusion | flops 262144 | bytes 3145856 | tf_op jit(solution)/shard_map/scatter-add | solution.py:53
  25.9 1.4 convert_element_type.40
  27.3 0.0 copy-start.1
  27.3 5.5 %copy.13 = bf16[2,128,25,128]{1,0,3,2:T(2,128)(2,1)} copy(bf16[2,128,25,128]{3,1,2,0:T(8,128)(2,1)} %convert_element_type.40) | data formatting | bytes 3276800 | tf_op jit(solution)/shard_map/convert_element_type | solution.py:54
  32.8 59.8 %all-gather.2.cloned.1.call-done = bf16[256,2048]{1,0:T(8,128)(2,1)} async-done(((bf16[8,2048]{1,0:T(8,128)(2,1)}), bf16[256,2048]{1,0:T(8,128)(2,1)}) %all-gather.2.cloned.1.call-update) | async-done | bytes 1048592 | tf_op jit(solution)/shard_map/all_gather | solution.py:18
  92.7 0.0 copy-done.1
  92.7 0.0 copy-start
  92.7 3.1 %fusion.2 = f32[1024,3200]{1,0:T(8,128)S(1)} fusion(bf16[400,8,2,128]{3,2,1,0:T(2,128)(2,1)S(1)} %bitcast.25, bf16[256,2048]{1,0:T(8,128)(2,1)} %all-gather.2.cloned.1.call-done), kind=kOutput, calls=%fused_computation.5 | convolution fusion | flops 1677721600 | bytes 15269888 | tf_op jit(solution)/shard_map/dot_general | solution.py:95
  95.8 0.0 copy-done
  95.8 6.3 %add_convert_fusion = bf16[1024,3200]{1,0:T(8,128)(2,1)} fusion(f32[1024,3200]{1,0:T(8,128)S(1)} %fusion.2, bf16[400,8,2,128]{3,2,1,0:T(2,128)(2,1)} %bitcast.26, bf16[256,2048]{1,0:T(8,128)(2,1)S(1)} %copy-done), kind=kOutput, calls=%fused_computation.2 | convolution fusion | flops 1687552000 | bytes 21823488 | tf_op jit(solution)/shard_map/dot_general | solution.py:97
  102.1 0.0 reduce-scatter.3.cloned.1.call-update
  102.1 0.0 reduce-scatter.5.cloned.1.call-start
  102.1 65.4 %reduce-scatter.3.cloned.1.call-done = bf16[256,3200]{1,0:T(8,128)(2,1)} async-done(((bf16[1024,3200]{1,0:T(8,128)(2,1)}), bf16[256,3200]{1,0:T(8,128)(2,1)}) %reduce-scatter.3.cloned.1.call-update) | async-done | bytes 1638416 | tf_op jit(solution)/shard_map/reduce_scatter | solution.py:34
  167.5 0.0 reduce-scatter.5.cloned.1.call-update
  167.5 0.1 fusion.19
  167.6 0.3 fusion.9
  167.9 0.3 fusion.7
  168.3 0.6 copy.27
  168.9 3.4 %all-to-all-start = ((bf16[8,128,32]{1,2,0:T(8,128)(2,1)}), bf16[8,128,32]{1,2,0:T(8,128)(2,1)S(1)}, u32[]{:S(2)}, u32[]{:S(2)}) async-start(bf16[8,128,32]{1,2,0:T(8,128)(2,1)} %bitcast.24), calls=%async_computation.2 | async-start | bytes 131072 | tf_op jit(solution)/shard_map/all_to_all | solution.py:45
  172.3 0.2 multiply_reduce_fusion
  172.5 8.7 %psum.14 = f32[1024]{0:T(1024)S(1)} all-reduce(f32[1024]{0:T(1024)S(1)} %multiply_add_fusion), channel_id=1, replica_groups=mesh['user_0'=4,'user_1'=2,'item'=32] {'user_0'}, use_global_device_ids=true, to_apply=%region_6.0 | all-reduce | flops 1024 | bytes 8192 | tf_op jit(solution)/shard_map/psum | solution.py:27
  181.2 4.4 %psum.15 = f32[1024]{0:T(1024)S(1)} all-reduce(f32[1024]{0:T(1024)S(1)} %psum.14), channel_id=1, replica_groups=mesh['user_0'=4,'user_1'=2,'item'=32] {'user_1'}, use_global_device_ids=true, to_apply=%region_7.0 | all-reduce | flops 1024 | bytes 8192 | tf_op jit(solution)/shard_map/psum | solution.py:27
  185.6 0.1 add_rsqrt_fusion
  185.6 0.0 all-to-all-done
  185.7 0.7 multiply_select_fusion
  186.3 15.3 %reduce-scatter.5.cloned.1.call-done = bf16[128,3200]{1,0:T(8,128)(2,1)} async-done(((bf16[256,3200]{1,0:T(8,128)(2,1)}), bf16[128,3200]{1,0:T(8,128)(2,1)}) %reduce-scatter.5.cloned.1.call-update) | async-done | bytes 819216 | tf_op jit(solution)/shard_map/reduce_scatter | solution.py:34
  201.7 2.5 %convert_multiply_fusion = f32[128,3200]{1,0:T(8,128)} fusion(bf16[128,3200]{1,0:T(8,128)(2,1)} %reduce-scatter.5.cloned.1.call-done, f32[128]{0:T(128)S(1)} %add_rsqrt_fusion), kind=kLoop, calls=%fused_computation.8 | loop fusion | flops 819200 | bytes 2458112 | tf_op jit(solution)/shard_map/mul | solution.py:104
  (4 shorter events, 0.0 us)
Async XLA Ops:
  7.2 85.5 %all-gather.2.cloned.1.call-start = ((), (), s32[]{:S(2)}) async-start(), calls=%async_computation.3 | async-start | bytes 1081344 | tf_op jit(solution)/shard_map/all_gather | solution.py:18
  8.6 158.9 %reduce-scatter.3.cloned.1.call-start = ((), (), s32[]{:S(2)}) async-start(), calls=%async_computation.4 | async-start | bytes 8192000 | tf_op jit(solution)/shard_map/reduce_scatter | solution.py:34
  16.2 5.4 %copy-start.2 = (bf16[16,128,128]{2,1,0:T(8,128)(2,1)S(1)}, bf16[16,128,128]{2,1,0:T(8,128)(2,1)}, u32[]{:S(2)}) copy-start(bf16[16,128,128]{2,1,0:T(8,128)(2,1)} %param.13) | copy-start | bytes 1572868
  27.3 65.3 %copy-start.1 = (bf16[2,128,25,128]{1,0,3,2:T(2,128)(2,1)S(1)}, bf16[2,128,25,128]{1,0,3,2:T(2,128)(2,1)}, u32[]{:S(2)}) copy-start(bf16[2,128,25,128]{1,0,3,2:T(2,128)(2,1)} %copy.12) | copy-start | bytes 4915204
  92.7 3.1 %copy-start = (bf16[256,2048]{1,0:T(8,128)(2,1)S(1)}, bf16[256,2048]{1,0:T(8,128)(2,1)}, u32[]{:S(2)}) copy-start(bf16[256,2048]{1,0:T(8,128)(2,1)} %all-gather.2.cloned.1.call-done) | copy-start | bytes 3145732
  102.1 99.6 %reduce-scatter.5.cloned.1.call-start = ((), (), s32[]{:S(2)}) async-start(), calls=%async_computation.5 | async-start | bytes 2457600 | tf_op jit(solution)/shard_map/reduce_scatter | solution.py:34
  168.9 16.7 %all-to-all-start = ((bf16[8,128,32]{1,2,0:T(8,128)(2,1)}), bf16[8,128,32]{1,2,0:T(8,128)(2,1)S(1)}, u32[]{:S(2)}, u32[]{:S(2)}) async-start(bf16[8,128,32]{1,2,0:T(8,128)(2,1)} %bitcast.24), calls=%async_computation.2 | async-start | bytes 131072 | tf_op jit(solution)/shard_map/all_to_all | solution.py:45
Sparse Core Ops, SparseCore 0:
  10.8 81.8 all-gather.1
  102.2 65.2 reduce-scatter.2
  170.0 31.6 reduce-scatter.4
where the time goes:
time: 211 us
  waiting for transfers between devices  141 us (67%)
  other arithmetic  17.3 us (8%)
  between operations  13.9 us (7%)
  blocking collectives  13.1 us (6%)
  local copies, waits for them, and re-layouts  12.4 us (6%)
  matrix products  9.99 us (5%)
  starting transfers between devices  3.48 us (2%)
    reduce_scatter x2, waiting for transfers between devices, own_rows(): subtotal = lax.psum_scatter(subtotal, axis, scatter_dimension=0, tiled=True)  80.7 us
    all_gather x1, waiting for transfers between devices, sent_together(): result, at, outs = (lax.all_gather(both, axis, axis=dim, tiled=True), 0, [])  59.8 us
    psum x2, blocking collectives, over_axes(): value = lax.psum(value, axis)  13.1 us
    convert_element_type x2, local copies, waits for them, and re-layouts, dense_local(): return dense.reshape(row_blocks * side, item_width).astype(jnp.bfloat16)  10.9 us
    dot_general x1, matrix products, local(): lax.dot_general(attrs, attr_dense, contract, preferred_element_type=jnp.f...  6.25 us
    scatter-add x2, other arithmetic, dense_local(): dense = start.at[rows, :, cols, :].add(blocks.astype(jnp.float32))  5.74 us
  transfers between devices with their start and end apart: 4, of which 3 were waited for; matrix products, arithmetic and copies ran while one was open for 13% of the time, Pallas kernels for 0%

commit v1 on v0

v1 whole, which is shorter than its diff:
```python
import jax
import jax.numpy as jnp
from jax import lax
from jax.experimental import pallas as pl
from jax.experimental.pallas import tpu as pltpu
from jax.sharding import PartitionSpec as P

SIDE = 128
BLOCKS = 16
COLS = 25
ZERO = 64
NA, NB = 7, 6
NK = NA + NB
MESH = pl.DeviceIdType.MESH
F32, BF16 = jnp.float32, jnp.bfloat16


def merge_kernel(up, ap, ub, ab, ur, uc, ar, ac, u_out, blk_out, map_out, acc):
    for t, pan in enumerate((up, ap)):
        for m in range(8):
            u_out[m % 2, t, :, (m // 2) * 128:(m // 2 + 1) * 128] = pan[:, m * 128:(m + 1) * 128]
    for row in range(4):
        for c in range(COLS + 1):
            map_out[row, c] = ZERO
    for t, (blk, rows, cols) in enumerate(((ub, ur, uc), (ab, ar, ac))):
        twin = [jnp.int32(0)] * BLOCKS
        for q in range(BLOCKS - 1, -1, -1):
            row, c = t * 2 + rows[q, 0], cols[q, 0]
            twin[q] = map_out[row, c]
            map_out[row, c] = t * BLOCKS + q
        for q in range(BLOCKS):
            blk_out[t * BLOCKS + q] = blk[q]
        for q in range(BLOCKS - 1):
            row, c = t * 2 + rows[q, 0], cols[q, 0]
            first = jnp.logical_and(map_out[row, c] == t * BLOCKS + q, twin[q] != ZERO)

            @pl.when(first)
            def _(q=q, t=t, blk=blk, rows=rows, cols=cols):
                acc[...] = blk[q].astype(F32)

                def add(o, carry):
                    same = jnp.logical_and(rows[o, 0] == rows[q, 0], cols[o, 0] == cols[q, 0])

                    @pl.when(same)
                    def _():
                        acc[...] += blk[o].astype(F32)

                    return carry

                lax.fori_loop(q + 1, BLOCKS, add, 0)
                blk_out[t * BLOCKS + q] = acc[...].astype(BF16)


def gram_kernel(u_ref, blk_ref, map_ref, tail_ref, self_ref, w_ref,
                g, xb, smap, vmap, xrel, tall, pt, srhs, rhs,
                far, near_p, near_m, keep_p, keep_m, own, rfar_p, rfar_m, rp, rm,
                wrow, wsend, wrelay, wp, wm,
                loc, xs, xr, zs, zr, ss, sr, bs, br, es, er, fs, fr, ns, nr, vs, vr):
    user, item = lax.axis_index("user"), lax.axis_index("item")
    y, a = user // 2, user % 2
    z, h, c = item // 4, (item // 2) % 2, item % 2
    x = h * 2 + a

    def dev(dy=0, dx=0, dz=0, flip=False):
        yy, xx, zz = (y + dy + 4) % 4, (x + dx + 4) % 4, (z + dz + 8) % 8
        cc = 1 - c if flip else c
        return (yy * 2 + xx % 2, zz * 4 + (xx // 2) * 2 + cc)

    partner = (y * 2 + (1 - a), item)

    def send(src, dst, ssem, rsem, to):
        return pltpu.make_async_remote_copy(
            src_ref=src, dst_ref=dst, send_sem=ssem, recv_sem=rsem,
            device_id=to, device_id_type=MESH)

    barrier = pltpu.get_barrier_semaphore()
    for peer in (dev(dy=1), dev(dy=-1), dev(dx=1), dev(dx=-1), dev(dz=1), dev(dz=-1), dev(flip=True)):
        pl.semaphore_signal(barrier, inc=1, device_id=peer, device_id_type=MESH)
    pl.semaphore_wait(barrier, 7)

    h_left, h_right = ((x + 3) % 4) // 2, ((x + 1) % 4) // 2
    x_copies = [
        send(u_ref.at[1 - a], g.at[z, c, 1, h], xs.at[0], xr.at[0], dev(dx=1)),
        send(u_ref.at[1 - a], g.at[z, c, 1, h], xs.at[1], xr.at[1], dev(dx=-1)),
        send(u_ref.at[a, 0], xrel.at[0], xs.at[2], xr.at[2], dev(dx=1)),
        send(u_ref.at[a, 1], xrel.at[1], xs.at[3], xr.at[3], dev(dx=-1)),
    ]
    for cp in (x_copies[2], x_copies[3], x_copies[0], x_copies[1]):
        cp.start()
    map_copy = send(map_ref, vmap, bs.at[4], br.at[4], partner)
    map_copy.start()
    b_copies = [send(blk_ref.at[pl.ds(8 * i, 8)], xb.at[pl.ds(32 + 8 * i, 8)], bs.at[i], br.at[i], partner)
                for i in range(4)]
    for cp in b_copies:
        cp.start()
    own_u = pltpu.make_async_copy(u_ref.at[a], g.at[z, c, 0, h], loc.at[0])
    own_b = pltpu.make_async_copy(blk_ref, xb.at[pl.ds(0, 32)], loc.at[1])
    own_m = pltpu.make_async_copy(map_ref, smap.at[0], loc.at[2])
    for cp in (own_u, own_b, own_m):
        cp.start()
    xb[ZERO] = jnp.zeros((SIDE, SIDE), BF16)
    x_copies[2].wait_recv()
    fwd0 = send(xrel.at[0], g.at[z, c, 0, h_left, 0], xs.at[4], xr.at[4], dev(dx=1))
    fwd0.start()
    x_copies[3].wait_recv()
    fwd1 = send(xrel.at[1], g.at[z, c, 0, h_right, 1], xs.at[5], xr.at[5], dev(dx=-1))
    fwd1.start()
    x_copies[0].wait_recv()
    x_copies[1].wait_recv()

    def ring(step, sub, up):
        zz = (z + 8 - step) % 8 if up else (z + step) % 8
        i = (step if up else 4 + step) * 2 + sub
        return send(g.at[zz, c, sub], g.at[zz, c, sub], zs.at[i], zr.at[i], dev(dz=1 if up else -1))

    def share(zz, i):
        return send(g.at[zz, c], g.at[zz, c], ss.at[i], sr.at[i], dev(flip=True))

    ups = [[ring(k, s, True) for s in range(2)] for k in range(4)]
    downs = [[ring(k, s, False) for s in range(2)] for k in range(3)]
    ups[0][1].start()
    downs[0][1].start()
    own_u.wait()
    fwd0.wait_recv()
    fwd1.wait_recv()
    ups[0][0].start()
    downs[0][0].start()
    shares = [share(z, 0)]
    shares[0].start()
    for k in range(4):
        for s in (1, 0):
            ups[k][s].wait_recv()
            if k < 3:
                ups[k + 1][s].start()
                downs[k][s].wait_recv()
                if k < 2:
                    downs[k + 1][s].start()
        shares.append(share((z + 7 - k) % 8, 1 + k))
        shares[-1].start()
        if k < 3:
            shares.append(share((z + 1 + k) % 8, 5 + k))
            shares[-1].start()
    for cp in shares:
        cp.wait_recv()

    for rel in range(4):
        wrow[rel] = jnp.zeros((8, SIDE), F32)
    for side in range(2):
        for t in range(2):
            for i in range(32):
                tall[i * 8:(i + 1) * 8, :] = g[i // 4, i % 2, side, (i // 2) % 2, t].astype(F32)
            first = side * 512 + t * 256
            for rel in range(4):
                yb = (y + rel) % 4
                v = tall[:, pl.ds(pl.multiple_of(yb * SIDE, SIDE), SIDE)]
                squares = jnp.sum(v * v, axis=0, keepdims=True)
                vt = v.T
                if t == 1:
                    squares, vt = squares * 0.5, vt * 0.5
                wrow[rel] += jnp.broadcast_to(squares, (8, SIDE))
                pt[rel * SIDE:(rel + 1) * SIDE, first:first + 256] = vt.astype(BF16)

            @pl.when(z % 2 == a)
            def _():
                srhs[first:first + 256, :] = tall[:, pl.ds(pl.multiple_of((z // 2) * SIDE, SIDE), SIDE)].astype(BF16)

    wsend[0] = wrow[2]
    wsend[1] = wrow[3]
    w_far = send(wsend.at[0], wrelay, vs.at[0], vr.at[0], dev(dy=1))
    w_near_m = send(wsend.at[1], wm, vs.at[1], vr.at[1], dev(dy=-1))
    w_far.start()
    w_near_m.start()

    map_copy.wait_recv()
    got_map = pltpu.make_async_copy(vmap, smap.at[1], loc.at[3])
    got_map.start()
    own_b.wait()
    own_m.wait()
    got_map.wait()
    for cp in b_copies:
        cp.wait_recv()

    e_copies = [send(srhs.at[pl.ds(s * 512, 512)], srhs.at[pl.ds((1 - s) * 512, 512)], es.at[s], er.at[s], partner)
                for s in range(2)]

    @pl.when(z % 2 == a)
    def _():
        for cp in e_copies:
            cp.start()

    def far_copy(k, up):
        if up:
            return send(far.at[k], rfar_p.at[k], fs.at[k], fr.at[k], dev(dy=1))
        return send(far.at[k], rfar_m.at[k - NA], fs.at[k], fr.at[k], dev(dy=-1))

    def near_copy(k, up):
        if up:
            return send(near_p.at[k], rp.at[k], ns.at[k], nr.at[k], dev(dy=1))
        return send(near_m.at[k], rm.at[k], ns.at[NK + k], nr.at[NK + k], dev(dy=-1))

    def compute(k, up, last=False):
        for j in range(1 if last else 2):
            for p in range(8):
                at = smap[p // 4, p % 4, 2 * k + j]
                if p >= 4:
                    at = jnp.where(at == ZERO, ZERO, at + 32)
                rhs[p * SIDE:(p + 1) * SIDE, j * SIDE:(j + 1) * SIDE] = xb[at]
        if last:
            rhs[:, SIDE:2 * SIDE] = srhs[...]
        terms = jnp.dot(pt[...], rhs[...], preferred_element_type=F32)
        far[k] = terms[256:384].astype(BF16)
        far_copy(k, up).start()
        own[k] = terms[0:128]
        if up:
            near_m[k] = terms[384:512].astype(BF16)
            near_copy(k, False).start()
            keep_p[k] = terms[128:256]
        else:
            near_p[k] = terms[128:256].astype(BF16)
            near_copy(k, True).start()
            keep_m[k - NA] = terms[384:512]

    def both(i, carry):
        compute(i, True)
        compute(NA + i, False)
        return carry

    lax.fori_loop(0, NB - 1, both, 0)
    compute(NB - 1, True)
    compute(NA - 1, True)

    @pl.when(z % 2 != a)
    def _():
        for cp in e_copies:
            cp.wait_recv()

    compute(NK - 1, False, last=True)

    w_far.wait_recv()
    wsend[2] = wrow[1] + wrelay[...]
    w_near_p = send(wsend.at[2], wp, vs.at[2], vr.at[2], dev(dy=1))
    w_near_p.start()

    def relay_up(k):
        far_copy(k, True).wait_recv()
        near_p[k] = (keep_p[k] + rfar_p[k].astype(F32)).astype(BF16)
        near_copy(k, True).start()

    def relay_down(k):
        far_copy(k, False).wait_recv()
        near_m[k] = (keep_m[k - NA] + rfar_m[k - NA].astype(F32)).astype(BF16)
        near_copy(k, False).start()

    def relay(i, carry):
        relay_up(i)
        relay_down(NA + i)
        return carry

    lax.fori_loop(0, NB, relay, 0)
    relay_up(NA - 1)

    def total(k):
        near_copy(k, True).wait_recv()
        near_copy(k, False).wait_recv()
        return own[k] + (rp[k].astype(F32) + rm[k].astype(F32))

    def finish(k, carry):
        tail_ref[:, pl.ds(pl.multiple_of(k * 256, 256), 256)] = total(k)
        return carry

    lax.fori_loop(0, NK - 1, finish, 0)
    end = total(NK - 1)
    tail_ref[:, (NK - 1) * 256:] = end[:, :SIDE]
    self_ref[...] = end[:, SIDE:]
    w_near_m.wait_recv()
    w_near_p.wait_recv()
    w_ref[...] = wrow[0] + (wp[...] + wm[...])

    for cp in x_copies + [fwd0, fwd1] + shares + b_copies + [map_copy, w_far, w_near_m, w_near_p]:
        cp.wait_send()
    for cp in ups + downs:
        for part in cp:
            part.wait_send()

    @pl.when(z % 2 == a)
    def _():
        for cp in e_copies:
            cp.wait_send()

    def drain_a(k, carry):
        far_copy(k, True).wait_send()
        near_copy(k, True).wait_send()
        near_copy(k, False).wait_send()
        return carry

    def drain_b(k, carry):
        far_copy(k, False).wait_send()
        near_copy(k, True).wait_send()
        near_copy(k, False).wait_send()
        return carry

    lax.fori_loop(0, NA, drain_a, 0)
    lax.fori_loop(NA, NK, drain_b, 0)


def local(up, ap, ub, ur, uc, ab, ar, ac):
    vmem, smem = pl.BlockSpec(memory_space=pltpu.VMEM), pl.BlockSpec(memory_space=pltpu.SMEM)
    hbm = pl.BlockSpec(memory_space=pl.ANY)
    shape = jax.ShapeDtypeStruct
    u, blk, cells = pl.pallas_call(
        merge_kernel,
        out_shape=(shape((2, 2, 8, 512), BF16), shape((32, SIDE, SIDE), BF16), shape((8, 128), jnp.int32)),
        in_specs=[vmem] * 4 + [smem] * 4,
        out_specs=(vmem, vmem, smem),
        scratch_shapes=[pltpu.VMEM((SIDE, SIDE), F32)],
        name="merge",
    )(up, ap, ub, ab, ur, uc, ar, ac)
    vm, dma = pltpu.VMEM, pltpu.SemaphoreType.DMA
    width = (NK * 2 - 1) * SIDE
    tail, own_self, weight = pl.pallas_call(
        gram_kernel,
        out_shape=(shape((SIDE, width), F32), shape((SIDE, SIDE), F32), shape((8, SIDE), F32)),
        in_specs=[hbm, hbm, hbm],
        out_specs=(vmem, vmem, vmem),
        scratch_shapes=[
            vm((8, 2, 2, 2, 2, 8, 512), BF16),
            vm((ZERO + 1, SIDE, SIDE), BF16),
            pltpu.SMEM((2, 8, 128), jnp.int32),
            vm((8, 128), jnp.int32),
            vm((2, 8, 512), BF16),
            vm((256, 512), F32),
            vm((512, 1024), BF16),
            vm((1024, SIDE), BF16),
            vm((1024, 256), BF16),
            vm((NK, SIDE, 256), BF16),
            vm((NK, SIDE, 256), BF16),
            vm((NK, SIDE, 256), BF16),
            vm((NA, SIDE, 256), F32),
            vm((NB, SIDE, 256), F32),
            vm((NK, SIDE, 256), F32),
            vm((NA, SIDE, 256), BF16),
            vm((NB, SIDE, 256), BF16),
            vm((NK, SIDE, 256), BF16),
            vm((NK, SIDE, 256), BF16),
            vm((4, 8, SIDE), F32),
            vm((3, 8, SIDE), F32),
            vm((8, SIDE), F32),
            vm((8, SIDE), F32),
            vm((8, SIDE), F32),
            dma((4,)), dma((6,)), dma((6,)), dma((14,)), dma((14,)), dma((8,)), dma((8,)),
            dma((5,)), dma((5,)), dma((2,)), dma((2,)), dma((NK,)), dma((NK,)),
            dma((2 * NK,)), dma((2 * NK,)), dma((3,)), dma((3,)),
        ],
        compiler_params=pltpu.CompilerParams(
            collective_id=0, has_side_effects=True, vmem_limit_bytes=48 * 1024 * 1024),
        name="gram",
    )(u, blk, cells)
    user, item = lax.axis_index("user"), lax.axis_index("item")
    scale = lax.rsqrt(weight[0] + 1.0)[:, None]
    part = lax.dynamic_slice_in_dim(own_self, (item % 4) * 32, 32, 1)
    rows = user * SIDE + lax.broadcasted_iota(jnp.int32, part.shape, 0)
    cols = item * 32 + lax.broadcasted_iota(jnp.int32, part.shape, 1)
    return tail * scale, jnp.where(rows == cols, jnp.float32(0.0), part * scale)


def solution(mesh):
    both = P(("user", "item"), None)
    return jax.shard_map(
        local,
        mesh=mesh,
        in_specs=(both, both, P("user", "item", None), P("user", "item"), P("user", "item"),
                  P("user", "item", None), P("user", "item"), P("user", "item")),
        out_specs=(P("user", "item"), P("user", "item")),
        check_vma=False,
    )
```

time: 211 us -> 96 us (0.45)
  waiting for transfers between devices: 141 us -> 0 us
  Pallas kernels: 0 us -> 84.8 us
  other arithmetic: 17.3 us -> 1.47 us
  between operations: 13.9 us -> 0.71 us
  blocking collectives: 13.1 us -> 0 us
  matrix products: 9.99 us -> 0 us
  local copies, waits for them, and re-layouts: 12.4 us -> 8.64 us
  starting transfers between devices: 3.48 us -> 0 us
    pallas_call x0 -> x2, Pallas kernels: none -> 84.8 us  [the longest x1 81.7 us: local(): pl.pallas_call(gram_kernel, out_shape=(shape((SIDE, width), F32), shape((...]
    reduce_scatter x2 -> x0, waiting for transfers between devices: 80.7 us -> none  [own_rows(): subtotal = lax.psum_scatter(subtotal, axis, scatter_dimension=0, tiled=True)]
    all_gather x1 -> x0, waiting for transfers between devices: 59.8 us -> none  [sent_together(): result, at, outs = (lax.all_gather(both, axis, axis=dim, tiled=True), 0, [])]
    psum x2 -> x0, blocking collectives: 13.1 us -> none  [over_axes(): value = lax.psum(value, axis)]
    convert_element_type x2 -> x0, local copies, waits for them, and re-layouts: 10.9 us -> none  [dense_local(): return dense.reshape(row_blocks * side, item_width).astype(jnp.bfloat16)]
    dot_general x4 -> x0, matrix products: 9.99 us -> none  [the longest x1 6.25 us: local(): lax.dot_general(attrs, attr_dense, contract, preferred_element_type=jnp.f...]
    unnamed x6 -> x11, local copies, waits for them, and re-layouts: 0.01 us -> 8.64 us
    convert_element_type x4 -> x0, other arithmetic: 6.06 us -> none  [the longest x2 3.19 us: dense_local(): dense = start.at[rows, :, cols, :].add(blocks.astype(jnp.float32))]
  transfers between devices with their start and end apart: 4 -> 0, of which waited for: 3 -> 0; matrix products, arithmetic and copies ran while one was open for 13% -> 0% of each run, Pallas kernels for 0% -> 0%
where the time goes in v1:
time: 96 us; the launch traced here: 95.6 us
  Pallas kernels  84.8 us (88%)
  local copies, waits for them, and re-layouts  8.64 us (9%)
  other arithmetic  1.47 us (2%)
    pallas_call x1, Pallas kernels, local(): pl.pallas_call(gram_kernel, out_shape=(shape((SIDE, width), F32), shape((...  81.7 us
    unnamed x11, local copies, waits for them, and re-layouts  8.64 us
    pallas_call x1, Pallas kernels, local(): pl.pallas_call(merge_kernel, out_shape=(shape((2, 2, 8, 512), BF16), shap...  3.05 us

profile of v1, /device:TPU:1, one launch (start us, length us, event | category | flops | bytes accessed | tf_op | source)
XLA Modules:
  0.0 95.6 jit_solution(17946083464393132055)
XLA Ops:
  0.7 1.3 %copy.10.ur = s32[16,1]{1,0:T(8,128)} copy(s32[16,1]{0,1:T(1,128)} %param.11) | data formatting | bytes 128 | tf_op args[3]
  2.0 1.3 %copy.11.uc = s32[16,1]{1,0:T(8,128)} copy(s32[16,1]{0,1:T(1,128)} %param.12) | data formatting | bytes 128 | tf_op args[4]
  3.3 1.3 %copy.12.ar = s32[16,1]{1,0:T(8,128)} copy(s32[16,1]{0,1:T(1,128)} %param.14) | data formatting | bytes 128 | tf_op args[6]
  4.7 1.3 %copy.13.ac = s32[16,1]{1,0:T(8,128)} copy(s32[16,1]{0,1:T(1,128)} %param.15) | data formatting | bytes 128 | tf_op args[7]
  6.0 3.1 %merge.1 = (bf16[2,2,8,512]{3,2,1,0:T(8,128)(2,1)}, bf16[32,128,128]{2,1,0:T(8,128)(2,1)}, s32[8,128]{1,0:T(8,128)}) custom-call(bf16[8,1024]{1,0:T(8,128)(2,1)} %up.1, bf16[8,1024]{1,0:T(8,128)(2,1)} %ap.1, bf16[16,128,128]{2,1,0:T(8,128)(2,1)} %ub.1, bf16[16,128,128]{2,1,0:T(8,128)(2,1)} %ab.1, s32[16,1]{1,0:T(8,128)} %copy.10.ur, s32[16,1]{1,0:T(8,128)} %copy.11.uc, ...), custom_call_target="tpu_custom_call" | custom-call | tf_op jit(solution)/shard_map/merge/pallas_call | solution.py:310
  9.1 0.0 copy-start
  9.1 1.2 %copy-done = bf16[32,128,128]{2,1,0:T(8,128)(2,1)S(1)} copy-done((bf16[32,128,128]{2,1,0:T(8,128)(2,1)S(1)}, bf16[32,128,128]{2,1,0:T(8,128)(2,1)}, u32[]{:S(2)}) %copy-start) | copy-done | bytes 1048600
  10.3 0.0 copy-start.1
  10.3 0.8 copy-done.1
  11.0 0.0 copy-start.2
  11.0 0.7 copy-done.2
  11.7 81.7 %gram.1 = (f32[128,3200]{1,0:T(8,128)S(1)}, f32[128,128]{1,0:T(8,128)S(1)}, f32[8,128]{1,0:T(8,128)S(1)}) custom-call(bf16[2,2,8,512]{3,2,1,0:T(8,128)(2,1)S(1)} %copy-done.1, bf16[32,128,128]{2,1,0:T(8,128)(2,1)S(1)} %copy-done, s32[8,128]{1,0:T(8,128)S(1)} %copy-done.2), custom_call_target="tpu_custom_call" | custom-call | tf_op jit(solution)/shard_map/gram/pallas_call | solution.py:320
  93.5 0.1 multiply_select_fusion
  93.6 0.7 copy.14
  94.3 1.3 %broadcast_multiply_fusion = f32[128,3200]{1,0:T(8,128)} fusion(f32[128,3200]{1,0:T(8,128)S(1)} %get-tuple-element.11, f32[128]{0:T(128)S(1)} %rsqrt_bitcast_fusion), kind=kLoop, calls=%fused_computation | loop fusion | flops 409600 | bytes 3277312 | tf_op jit(solution)/shard_map/mul | solution.py:363
  (3 shorter events, 0.0 us)
Async XLA Ops:
  9.1 1.2 %copy-start = (bf16[32,128,128]{2,1,0:T(8,128)(2,1)S(1)}, bf16[32,128,128]{2,1,0:T(8,128)(2,1)}, u32[]{:S(2)}) copy-start(bf16[32,128,128]{2,1,0:T(8,128)(2,1)} %get-tuple-element.9.blk_ref) | copy-start | bytes 3145732
  10.3 0.8 copy-start.1
  11.0 0.7 copy-start.2

commit v2 on v1

--- a/solution.py
+++ b/solution.py
@@ -25,13 +25,13 @@
     for t, (blk, rows, cols) in enumerate(((ub, ur, uc), (ab, ar, ac))):
         twin = [jnp.int32(0)] * BLOCKS
         for q in range(BLOCKS - 1, -1, -1):
-            row, c = t * 2 + rows[q, 0], cols[q, 0]
+            row, c = t * 2 + rows[0, q], cols[0, q]
             twin[q] = map_out[row, c]
             map_out[row, c] = t * BLOCKS + q
         for q in range(BLOCKS):
             blk_out[t * BLOCKS + q] = blk[q]
         for q in range(BLOCKS - 1):
-            row, c = t * 2 + rows[q, 0], cols[q, 0]
+            row, c = t * 2 + rows[0, q], cols[0, q]
             first = jnp.logical_and(map_out[row, c] == t * BLOCKS + q, twin[q] != ZERO)
 
             @pl.when(first)
@@ -39,7 +39,7 @@
                 acc[...] = blk[q].astype(F32)
 
                 def add(o, carry):
-                    same = jnp.logical_and(rows[o, 0] == rows[q, 0], cols[o, 0] == cols[q, 0])
+                    same = jnp.logical_and(rows[0, o] == rows[0, q], cols[0, o] == cols[0, q])
 
                     @pl.when(same)
                     def _():
@@ -52,7 +52,7 @@
 
 
 def gram_kernel(u_ref, blk_ref, map_ref, tail_ref, self_ref, w_ref,
-                g, xb, smap, vmap, xrel, tall, pt, srhs, rhs,
+                g, xb, smap, vmap, tall, pt, srhs, rhs,
                 far, near_p, near_m, keep_p, keep_m, own, rfar_p, rfar_m, rp, rm,
                 wrow, wsend, wrelay, wp, wm,
                 loc, xs, xr, zs, zr, ss, sr, bs, br, es, er, fs, fr, ns, nr, vs, vr):
@@ -74,18 +74,16 @@
             device_id=to, device_id_type=MESH)
 
     barrier = pltpu.get_barrier_semaphore()
-    for peer in (dev(dy=1), dev(dy=-1), dev(dx=1), dev(dx=-1), dev(dz=1), dev(dz=-1), dev(flip=True)):
+    for peer in (dev(dy=1), dev(dy=-1), dev(dx=1), dev(dx=-1), dev(dx=2), dev(dz=1), dev(dz=-1), dev(flip=True)):
         pl.semaphore_signal(barrier, inc=1, device_id=peer, device_id_type=MESH)
-    pl.semaphore_wait(barrier, 7)
-
-    h_left, h_right = ((x + 3) % 4) // 2, ((x + 1) % 4) // 2
+    pl.semaphore_wait(barrier, 8)
+
     x_copies = [
+        send(u_ref.at[a], g.at[z, c, 0, h], xs.at[2], xr.at[2], dev(dx=2)),
         send(u_ref.at[1 - a], g.at[z, c, 1, h], xs.at[0], xr.at[0], dev(dx=1)),
         send(u_ref.at[1 - a], g.at[z, c, 1, h], xs.at[1], xr.at[1], dev(dx=-1)),
-        send(u_ref.at[a, 0], xrel.at[0], xs.at[2], xr.at[2], dev(dx=1)),
-        send(u_ref.at[a, 1], xrel.at[1], xs.at[3], xr.at[3], dev(dx=-1)),
     ]
-    for cp in (x_copies[2], x_copies[3], x_copies[0], x_copies[1]):
+    for cp in x_copies:
         cp.start()
     map_copy = send(map_ref, vmap, bs.at[4], br.at[4], partner)
     map_copy.start()
@@ -99,14 +97,8 @@
     for cp in (own_u, own_b, own_m):
         cp.start()
     xb[ZERO] = jnp.zeros((SIDE, SIDE), BF16)
+    x_copies[1].wait_recv()
     x_copies[2].wait_recv()
-    fwd0 = send(xrel.at[0], g.at[z, c, 0, h_left, 0], xs.at[4], xr.at[4], dev(dx=1))
-    fwd0.start()
-    x_copies[3].wait_recv()
-    fwd1 = send(xrel.at[1], g.at[z, c, 0, h_right, 1], xs.at[5], xr.at[5], dev(dx=-1))
-    fwd1.start()
-    x_copies[0].wait_recv()
-    x_copies[1].wait_recv()
 
     def ring(step, sub, up):
         zz = (z + 8 - step) % 8 if up else (z + step) % 8
@@ -121,8 +113,7 @@
     ups[0][1].start()
     downs[0][1].start()
     own_u.wait()
-    fwd0.wait_recv()
-    fwd1.wait_recv()
+    x_copies[0].wait_recv()
     ups[0][0].start()
     downs[0][0].start()
     shares = [share(z, 0)]
@@ -276,7 +267,7 @@
     w_near_p.wait_recv()
     w_ref[...] = wrow[0] + (wp[...] + wm[...])
 
-    for cp in x_copies + [fwd0, fwd1] + shares + b_copies + [map_copy, w_far, w_near_m, w_near_p]:
+    for cp in x_copies + shares + b_copies + [map_copy, w_far, w_near_m, w_near_p]:
         cp.wait_send()
     for cp in ups + downs:
         for part in cp:
@@ -314,7 +305,7 @@
         out_specs=(vmem, vmem, smem),
         scratch_shapes=[pltpu.VMEM((SIDE, SIDE), F32)],
         name="merge",
-    )(up, ap, ub, ab, ur, uc, ar, ac)
+    )(up, ap, ub, ab, ur.T, uc.T, ar.T, ac.T)
     vm, dma = pltpu.VMEM, pltpu.SemaphoreType.DMA
     width = (NK * 2 - 1) * SIDE
     tail, own_self, weight = pl.pallas_call(
@@ -327,7 +318,6 @@
             vm((ZERO + 1, SIDE, SIDE), BF16),
             pltpu.SMEM((2, 8, 128), jnp.int32),
             vm((8, 128), jnp.int32),
-            vm((2, 8, 512), BF16),
             vm((256, 512), F32),
             vm((512, 1024), BF16),
             vm((1024, SIDE), BF16),
@@ -347,12 +337,12 @@
             vm((8, SIDE), F32),
             vm((8, SIDE), F32),
             vm((8, SIDE), F32),
-            dma((4,)), dma((6,)), dma((6,)), dma((14,)), dma((14,)), dma((8,)), dma((8,)),
+            dma((4,)), dma((3,)), dma((3,)), dma((14,)), dma((14,)), dma((8,)), dma((8,)),
             dma((5,)), dma((5,)), dma((2,)), dma((2,)), dma((NK,)), dma((NK,)),
             dma((2 * NK,)), dma((2 * NK,)), dma((3,)), dma((3,)),
         ],
         compiler_params=pltpu.CompilerParams(
-            collective_id=0, has_side_effects=True, vmem_limit_bytes=48 * 1024 * 1024),
+            collective_id=0, has_side_effects=True, vmem_limit_bytes=62 * 1024 * 1024),
         name="gram",
     )(u, blk, cells)
     user, item = lax.axis_index("user"), lax.axis_index("item")

time: 96 us -> 77.7 us (0.81)
  Pallas kernels: 84.8 us -> 71.7 us
  local copies, waits for them, and re-layouts: 8.64 us -> 0.68 us
  other arithmetic: 1.47 us -> 4.42 us
    pallas_call x1, Pallas kernels: 81.7 us -> 68.4 us  [local(): pl.pallas_call(gram_kernel, out_shape=(shape((SIDE, width), F32), shape((...]
    unnamed x11 -> x1, local copies, waits for them, and re-layouts: 8.64 us -> 0.68 us
    mul x1, other arithmetic: 1.34 us -> 2.77 us  [local(): tail * scale]
where the time goes in v2:
time: 77.7 us; the launch traced here: 77.5 us
  Pallas kernels  71.7 us (92%)
  other arithmetic  4.42 us (6%)
    pallas_call x1, Pallas kernels, local(): pl.pallas_call(gram_kernel, out_shape=(shape((SIDE, width), F32), shape((...  68.4 us
    pallas_call x1, Pallas kernels, local(): pl.pallas_call(merge_kernel, out_shape=(shape((2, 2, 8, 512), BF16), shap...  3.25 us
    mul x1, other arithmetic, local(): tail * scale  2.77 us

profile of v2, /device:TPU:1, one launch (start us, length us, event | category | flops | bytes accessed | tf_op | source)
XLA Modules:
  0.0 77.5 jit_solution(12371779494090707057)
XLA Ops:
  0.7 3.2 %merge.1 = (bf16[2,2,8,512]{3,2,1,0:T(8,128)(2,1)}, bf16[32,128,128]{2,1,0:T(8,128)(2,1)}, s32[8,128]{1,0:T(8,128)}) custom-call(bf16[8,1024]{1,0:T(8,128)(2,1)} %up.1, bf16[8,1024]{1,0:T(8,128)(2,1)} %ap.1, bf16[16,128,128]{2,1,0:T(8,128)(2,1)} %ub.1, bf16[16,128,128]{2,1,0:T(8,128)(2,1)} %ab.1, s32[1,16]{1,0:T(1,128)} %bitcast.6, s32[1,16]{1,0:T(1,128)} %bitcast.7, ...), custom_call_target="tpu_custom_call" | custom-call | tf_op jit(solution)/shard_map/merge/pallas_call | solution.py:301
  3.9 68.4 %gram.1 = (f32[128,3200]{1,0:T(8,128)}, f32[128,128]{1,0:T(8,128)}, f32[8,128]{1,0:T(8,128)}) custom-call(bf16[2,2,8,512]{3,2,1,0:T(8,128)(2,1)} %get-tuple-element.8.u_ref, bf16[32,128,128]{2,1,0:T(8,128)(2,1)} %get-tuple-element.9.blk_ref, s32[8,128]{1,0:T(8,128)} %get-tuple-element.10.map_ref), custom_call_target="tpu_custom_call" | custom-call | tf_op jit(solution)/shard_map/gram/pallas_call | solution.py:311
  72.4 0.7 rsqrt_bitcast_fusion
  73.0 1.0 %multiply_select_fusion = f32[128,32]{1,0:T(8,128)S(1)} fusion(f32[128,128]{1,0:T(8,128)} %get-tuple-element.13, s32[]{:T(128)S(6)} %select_n.15, f32[128]{0:T(128)S(1)} %rsqrt_bitcast_fusion, s32[32]{0:T(128)S(1)} %iota_add_fusion, s32[128]{0:T(128)S(1)} %iota_add_fusion.1), kind=kLoop, calls=%fused_computation.1 | loop fusion | flops 12288 | bytes 33924 | tf_op jit(solution)/shard_map/jit(_where)/select_n | solution.py:353
  74.0 0.7 copy.10
  74.7 2.8 %broadcast_multiply_fusion = f32[128,3200]{1,0:T(8,128)} fusion(f32[128,3200]{1,0:T(8,128)} %get-tuple-element.11, f32[128]{0:T(128)S(1)} %rsqrt_bitcast_fusion), kind=kLoop, calls=%fused_computation | loop fusion | flops 409600 | bytes 3277312 | tf_op jit(solution)/shard_map/mul | solution.py:353
  (2 shorter events, 0.0 us)
